TPU v7x, 32 devices: a whole 2x2x4 slice. The times are simulated.
32 devices in a mesh: curve: 8 (over z, x), sub: 4 (over y, core).
Axes of the slice: x: 2, y: 2, z: 4, core: 2. Of those that a mesh axis runs over, the one named last changes fastest.
Arguments:
- load: float32 [3, 32, 64, 128], P(None, 'sub', 'curve'), may hold values from -6 to 6
- plastic: float32 [32, 64, 128], P('sub', 'curve'), may hold values from 0 to 0.95, as said below
- tile_material: int32 [4, 8, 16], P('sub', 'curve'), may hold values from 0 to 4
- moduli: float32 [4], replicated, may hold values from 0.5 to 4
- k_vol: float32 [24, 24], replicated
- k_dev: float32 [24, 24], replicated
Outputs:
- solution: float32 [3, 32, 64, 128], P(None, 'sub', 'curve')
- residual: float32 [3, 32, 64, 128], P(None, 'sub', 'curve')
Inputs may be any that keep to these rules, and one draw needn't show every extreme that they name: `plastic`: zero for voxels that have not yielded, else the share lost.
All inputs are finite; a program needn't handle non-finite values.
Results may differ from a plain program's by a relative error of at most 0.0003.
Values sent between devices are 32-bit elements; how exact they have to be, the bound alone decides.
No kernel may reach another device: no remote copies, remote signals or barrier semaphores. Data moves between devices by JAX's collectives and lax.ppermute only.
A program may use at most 64 MiB of HBM per device.

v0:
```python
import jax
import jax.numpy as jnp
from jax import lax
from jax.sharding import PartitionSpec as P

TILE = 8
MATERIALS = 4
ITERS = 3
ground_spring = 0.5


def shifted(value, axis, by):
    count = lax.axis_size(axis)
    pairs = [(i, i + by) for i in range(count) if 0 <= i + by < count]
    return lax.ppermute(value, axis, pairs)


def padded(block, sides, width):
    for axis, dim in sides:
        count = lax.axis_size(axis)
        forward = [(i, i + 1) for i in range(count - 1)]
        backward = [(target, source) for source, target in forward]
        low = lax.ppermute(
            lax.slice_in_dim(block, block.shape[dim] - width, None, axis=dim), axis, forward
        )
        high = lax.ppermute(lax.slice_in_dim(block, 0, width, axis=dim), axis, backward)
        block = jnp.concatenate([low, block, high], axis=dim)
    return block


def voxel_coefficients(tile_material, moduli, plastic):
    one_hot = (tile_material[..., None] == jnp.arange(1, MATERIALS + 1, dtype=jnp.int32)).astype(
        jnp.float32
    )
    tile_modulus = jnp.sum(one_hot * moduli, axis=-1)
    voxel_modulus = jnp.repeat(jnp.repeat(jnp.repeat(tile_modulus, TILE, 0), TILE, 1), TILE, 2)
    return jnp.stack([voxel_modulus, voxel_modulus * (1.0 - plastic)])


def shift_second(values, along_y):
    if along_y == 0:
        return values
    zeros_col = jnp.zeros(values.shape[:-1] + (1,), values.dtype)
    return jnp.concatenate([zeros_col, values[..., :-1]], axis=-1)


def keep_mask(extended, first_x, first_z):
    size_x = extended.shape[1] - 1
    size_z = extended.shape[2] - 1
    size_y = extended.shape[3]
    occupied = (extended[0] > 0).astype(jnp.float32)
    active = jnp.zeros((size_x, size_z, size_y), jnp.float32)
    for along_x in (0, 1):
        for along_z in (0, 1):
            for along_y in (0, 1):
                contrib = occupied[
                    1 - along_x : 1 - along_x + size_x, 1 - along_z : 1 - along_z + size_z, :
                ]
                active = jnp.maximum(active, shift_second(contrib, along_y))
    index_x = first_x + jnp.arange(size_x, dtype=jnp.int32)
    index_z = first_z + jnp.arange(size_z, dtype=jnp.int32)
    index_y = jnp.arange(size_y, dtype=jnp.int32)
    free = (
        (index_x > 0)[:, None, None] & (index_z > 0)[None, :, None] & (index_y > 0)[None, None, :]
    )
    return active * free.astype(jnp.float32)


def node_forces(bordered, extended, k_vol, k_dev):
    size_x = extended.shape[1] - 1
    size_z = extended.shape[2] - 1
    size_y = extended.shape[3]
    lower = jnp.moveaxis(bordered[:, 0 : size_x + 1], 1, 0)
    upper = jnp.moveaxis(bordered[:, 1 : size_x + 2], 1, 0)
    layer_coef = jnp.moveaxis(extended, 1, 0)
    k_both = jnp.concatenate([k_vol, k_dev], axis=1)

    def assemble(forces, along_x):
        summed = jnp.zeros((3, size_z, size_y), jnp.float32)
        for along_z in (0, 1):
            for along_y in (0, 1):
                contrib = forces[along_x * 4 + along_z * 2 + along_y][
                    :, 1 - along_z : 1 - along_z + size_z, :
                ]
                summed = summed + shift_second(contrib, along_y)
        return summed

    def layer(carried, layer_item):
        lower_nodes, upper_nodes, coef_layer = layer_item
        corners = []
        for source in (lower_nodes, upper_nodes):
            for along_z in (0, 1):
                block = source[:, along_z : along_z + size_z + 1, :]
                corners.append(block)
                zeros_col = jnp.zeros((3, size_z + 1, 1), jnp.float32)
                corners.append(jnp.concatenate([block[:, :, 1:], zeros_col], axis=2))
        element = jnp.concatenate(corners, 0).reshape(24, (size_z + 1) * size_y)
        vol_scale = coef_layer[0].reshape(1, -1)
        dev_scale = coef_layer[1].reshape(1, -1)
        scaled = jnp.concatenate([vol_scale * element, dev_scale * element], axis=0)
        forces = jnp.dot(
            k_both, scaled, precision=lax.Precision.HIGHEST, preferred_element_type=jnp.float32
        )
        forces = forces.reshape(8, 3, size_z + 1, size_y)
        return (assemble(forces, 1), carried + assemble(forces, 0))

    start = jnp.zeros((3, size_z, size_y), jnp.float32)
    _, emitted = lax.scan(layer, start, (lower, upper, layer_coef))
    return jnp.moveaxis(emitted[1:], 0, 1)


def inner_sums(residual, image):
    return lax.psum((jnp.sum(residual * residual), jnp.sum(residual * image)), ("curve", "sub"))


def local(load, plastic, tile_material, moduli, k_vol, k_dev):
    coefficients = voxel_coefficients(tile_material, moduli, plastic)
    below_x = shifted(coefficients[:, -1:], "sub", 1)
    extended = jnp.concatenate([below_x, coefficients], axis=1)
    below_z = shifted(extended[:, :, -1:], "curve", 1)
    extended = jnp.concatenate([below_z, extended], axis=2)
    first_x = lax.axis_index("sub") * coefficients.shape[1]
    first_z = lax.axis_index("curve") * coefficients.shape[2]
    keep = keep_mask(extended, first_x, first_z)

    def operate(field_vals):
        bordered = padded(field_vals, (("curve", 2), ("sub", 1)), 1)
        return keep * (node_forces(bordered, extended, k_vol, k_dev) + ground_spring * field_vals)

    residual = keep * load
    solution = jnp.zeros_like(residual)
    image = operate(residual)
    norm_now, curvature = inner_sums(residual, image)
    step_size = norm_now / curvature
    direction = residual
    carried = image
    for iteration in range(ITERS):
        solution = solution + step_size * direction
        residual = residual - step_size * carried
        if iteration + 1 < ITERS:
            image = operate(residual)
            norm_next, curvature = inner_sums(residual, image)
            next_ratio = norm_next / norm_now
            step_size = norm_next / (curvature - next_ratio * norm_next / step_size)
            direction = residual + next_ratio * direction
            carried = image + next_ratio * carried
            norm_now = norm_next
    return (solution, residual)


def solution(mesh):
    in_specs = (
        P(None, "sub", "curve", None),
        P("sub", "curve", None),
        P("sub", "curve", None),
        P(),
        P(),
        P(),
    )
    out_specs = (P(None, "sub", "curve", None), P(None, "sub", "curve", None))
    return jax.shard_map(local, mesh=mesh, in_specs=in_specs, out_specs=out_specs, check_vma=False)
```

profile of v0, /device:TPU:0, one launch (start us, length us, event | category | flops | bytes accessed | tf_op | source)
XLA Modules:
  0.0 229.4 jit_solution(9882357935380456547)
XLA Ops:
  2.4 2.4 %collective-permute-start = (f32[2,1,8,128]{3,2,0,1:T(8,128)S(1)}, f32[2,1,8,128]{3,2,0,1:T(8,128)S(1)}, u32[]{:S(2)}, u32[]{:S(2)}) collective-permute-start(f32[2,1,8,128]{3,2,0,1:T(8,128)S(1)} %pad_maximum_fusion.12), channel_id=1, source_target_pairs={{0,1},{1,2},{2,3},{4,5},{5,6},{6,7},{8,9},{9,10},{10,11},{12,13},{... | collective-permute-start | bytes 24584 | tf_op jit(solution)/shard_map/ppermute | solution.py:15
  5.6 4.2 %collective-permute-start.1 = (f32[2,9,1,128]{3,2,0,1:T(1,128)S(1)}, f32[2,9,1,128]{3,2,0,1:T(1,128)S(1)}, u32[]{:S(2)}, u32[]{:S(2)}) collective-permute-start(f32[2,9,1,128]{3,2,0,1:T(1,128)S(1)} %pad_maximum_fusion.10), channel_id=1, source_target_pairs={{0,4},{4,8},{8,12},{12,16},{16,20},{20,24},{24,28},{1,5},{5,9},{9,... | collective-permute-start | bytes 27656 | tf_op jit(solution)/shard_map/ppermute | solution.py:15
  9.8 1.3 collective-permute-done.1
  12.2 4.2 %collective-permute-start.2 = (f32[3,8,1,128]{3,2,1,0:T(1,128)S(1)}, f32[3,8,1,128]{3,2,1,0:T(1,128)S(1)}, u32[]{:S(2)}, u32[]{:S(2)}) collective-permute-start(f32[3,8,1,128]{3,2,1,0:T(1,128)S(1)} %get-tuple-element.379), channel_id=1, source_target_pairs={{0,4},{4,8},{8,12},{12,16},{16,20},{20,24},{24,28},{1,5},{5,9},{9,... | collective-permute-start | bytes 36872 | tf_op jit(solution)/shard_map/ppermute | solution.py:23
  16.4 1.3 collective-permute-start.3
  17.7 4.6 %collective-permute-done.3 = f32[3,8,1,128]{3,2,1,0:T(1,128)S(1)} collective-permute-done((f32[3,8,1,128]{3,2,1,0:T(1,128)S(1)}, f32[3,8,1,128]{3,2,1,0:T(1,128)S(1)}, u32[]{:S(2)}, u32[]{:S(2)}) %collective-permute-start.3) | collective-permute-done | bytes 12320 | tf_op jit(solution)/shard_map/ppermute | solution.py:26
  22.4 1.4 collective-permute-start.4
  23.8 1.3 collective-permute-start.5
  25.2 5.8 %collective-permute-done.5 = f32[3,1,10,128]{3,2,1,0:T(8,128)S(1)} collective-permute-done((f32[3,1,10,128]{3,2,1,0:T(8,128)S(1)}, f32[3,1,10,128]{3,2,1,0:T(8,128)S(1)}, u32[]{:S(2)}, u32[]{:S(2)}) %collective-permute-start.5) | collective-permute-done | bytes 15392 | tf_op jit(solution)/shard_map/ppermute | solution.py:26
  31.0 9.3 %while.39 = (s32[]{:T(128)}, f32[3,8,128]{2,1,0:T(8,128)S(1)}, f32[9,3,8,128]{3,2,0,1:T(8,128)S(1)}, f32[9,2,9,128]{3,2,1,0:T(8,128)S(1)}, f32[9,3,10,128]{3,2,0...) while((s32[]{:T(128)}, f32[3,8,128]{2,1,0:T(8,128)S(1)}, ...), condition=%wide.region_4.5_spmd.clone, body=%wide.region_3.4_spmd.clone.sunk | while | flops 16060420 | bytes 1924459 | solution.py:108
  40.9 43.1 %all-reduce.30 = (f32[]{:T(128)}, f32[]{:T(128)}) all-reduce(f32[]{:T(128)} %get-tuple-element.256, f32[]{:T(128)} %get-tuple-element.255), channel_id=1, replica_groups=mesh['curve'=8,'sub'=4] {'curve','sub'}, use_global_device_ids=true, to_apply=%region_2.3 | all-reduce | flops 2 | bytes 16 | tf_op jit(solution)/shard_map/psum | solution.py:113
  85.5 4.2 %collective-permute-start.6 = (f32[3,8,1,128]{3,2,1,0:T(1,128)S(1)}, f32[3,8,1,128]{3,2,1,0:T(1,128)S(1)}, u32[]{:S(2)}, u32[]{:S(2)}) collective-permute-start(f32[3,8,1,128]{3,2,1,0:T(1,128)S(1)} %get-tuple-element.377), channel_id=1, source_target_pairs={{0,4},{4,8},{8,12},{12,16},{16,20},{20,24},{24,28},{1,5},{5,9},{9,... | collective-permute-start | bytes 36872 | tf_op jit(solution)/shard_map/ppermute | solution.py:23
  89.6 1.3 collective-permute-start.7
  91.0 4.2 %collective-permute-done.7 = f32[3,8,1,128]{3,2,1,0:T(1,128)S(1)} collective-permute-done((f32[3,8,1,128]{3,2,1,0:T(1,128)S(1)}, f32[3,8,1,128]{3,2,1,0:T(1,128)S(1)}, u32[]{:S(2)}, u32[]{:S(2)}) %collective-permute-start.7) | collective-permute-done | bytes 12320 | tf_op jit(solution)/shard_map/ppermute | solution.py:26
  96.5 1.3 collective-permute-start.9
  97.9 2.2 collective-permute-done.9
  100.2 9.3 %while.40 = (s32[]{:T(128)}, f32[3,8,128]{2,1,0:T(8,128)S(1)}, f32[9,3,8,128]{3,2,0,1:T(8,128)S(1)}, f32[9,2,9,128]{3,2,1,0:T(8,128)S(1)}, f32[9,3,10,128]{3,2,0...) while((s32[]{:T(128)}, f32[3,8,128]{2,1,0:T(8,128)S(1)}, ...), condition=%wide.region_10.11_spmd.clone, body=%wide.region_9.10_spmd.clone.sunk | while | flops 16060420 | bytes 1924459 | solution.py:108
  110.2 42.8 %all-reduce.29 = (f32[]{:T(128)}, f32[]{:T(128)}) all-reduce(f32[]{:T(128)} %get-tuple-element.254, f32[]{:T(128)} %get-tuple-element.253), channel_id=1, replica_groups=mesh['curve'=8,'sub'=4] {'curve','sub'}, use_global_device_ids=true, to_apply=%region_8.9 | all-reduce | flops 2 | bytes 16 | tf_op jit(solution)/shard_map/psum | solution.py:113
  157.4 4.2 %collective-permute-start.10 = (f32[3,8,1,128]{3,2,1,0:T(1,128)S(1)}, f32[3,8,1,128]{3,2,1,0:T(1,128)S(1)}, u32[]{:S(2)}, u32[]{:S(2)}) collective-permute-start(f32[3,8,1,128]{3,2,1,0:T(1,128)S(1)} %get-tuple-element.375), channel_id=1, source_target_pairs={{0,4},{4,8},{8,12},{12,16},{16,20},{20,24},{24,28},{1,5},{5,9},{9,... | collective-permute-start | bytes 36872 | tf_op jit(solution)/shard_map/ppermute | solution.py:23
  161.6 1.3 collective-permute-start.11
  163.0 4.2 %collective-permute-done.11 = f32[3,8,1,128]{3,2,1,0:T(1,128)S(1)} collective-permute-done((f32[3,8,1,128]{3,2,1,0:T(1,128)S(1)}, f32[3,8,1,128]{3,2,1,0:T(1,128)S(1)}, u32[]{:S(2)}, u32[]{:S(2)}) %collective-permute-start.11) | collective-permute-done | bytes 12320 | tf_op jit(solution)/shard_map/ppermute | solution.py:26
  169.8 2.3 collective-permute-done.13
  172.2 9.3 %while.41 = (s32[]{:T(128)}, f32[3,8,128]{2,1,0:T(8,128)S(1)}, f32[9,3,8,128]{3,2,0,1:T(8,128)S(1)}, f32[9,2,9,128]{3,2,1,0:T(8,128)S(1)}, f32[9,3,10,128]{3,2,0...) while((s32[]{:T(128)}, f32[3,8,128]{2,1,0:T(8,128)S(1)}, ...), condition=%wide.region_16.17_spmd.clone, body=%wide.region_15.16_spmd.clone.sunk | while | flops 16060420 | bytes 1924459 | solution.py:108
  182.1 42.8 %all-reduce.28 = (f32[]{:T(128)}, f32[]{:T(128)}) all-reduce(f32[]{:T(128)} %get-tuple-element.252, f32[]{:T(128)} %get-tuple-element.251), channel_id=1, replica_groups=mesh['curve'=8,'sub'=4] {'curve','sub'}, use_global_device_ids=true, to_apply=%region_14.15 | all-reduce | flops 2 | bytes 16 | tf_op jit(solution)/shard_map/psum | solution.py:113
  (841 shorter events, 33.9 us)
Async XLA Ops:
  0.6 0.7 copy-start.3
  0.7 0.7 copy-start.4
  2.4 3.2 %collective-permute-start = (f32[2,1,8,128]{3,2,0,1:T(8,128)S(1)}, f32[2,1,8,128]{3,2,0,1:T(8,128)S(1)}, u32[]{:S(2)}, u32[]{:S(2)}) collective-permute-start(f32[2,1,8,128]{3,2,0,1:T(8,128)S(1)} %pad_maximum_fusion.12), channel_id=1, source_target_pairs={{0,1},{1,2},{2,3},{4,5},{5,6},{6,7},{8,9},{9,10},{10,11},{12,13},{... | collective-permute-start | bytes 24584 | tf_op jit(solution)/shard_map/ppermute | solution.py:15
  5.6 5.6 %collective-permute-start.1 = (f32[2,9,1,128]{3,2,0,1:T(1,128)S(1)}, f32[2,9,1,128]{3,2,0,1:T(1,128)S(1)}, u32[]{:S(2)}, u32[]{:S(2)}) collective-permute-start(f32[2,9,1,128]{3,2,0,1:T(1,128)S(1)} %pad_maximum_fusion.10), channel_id=1, source_target_pairs={{0,4},{4,8},{8,12},{12,16},{16,20},{20,24},{24,28},{1,5},{5,9},{9,... | collective-permute-start | bytes 27656 | tf_op jit(solution)/shard_map/ppermute | solution.py:15
  11.2 0.9 copy-start
  12.2 5.6 %collective-permute-start.2 = (f32[3,8,1,128]{3,2,1,0:T(1,128)S(1)}, f32[3,8,1,128]{3,2,1,0:T(1,128)S(1)}, u32[]{:S(2)}, u32[]{:S(2)}) collective-permute-start(f32[3,8,1,128]{3,2,1,0:T(1,128)S(1)} %get-tuple-element.379), channel_id=1, source_target_pairs={{0,4},{4,8},{8,12},{12,16},{16,20},{20,24},{24,28},{1,5},{5,9},{9,... | collective-permute-start | bytes 36872 | tf_op jit(solution)/shard_map/ppermute | solution.py:23
  16.4 6.0 %collective-permute-start.3 = (f32[3,8,1,128]{3,2,1,0:T(1,128)S(1)}, f32[3,8,1,128]{3,2,1,0:T(1,128)S(1)}, u32[]{:S(2)}, u32[]{:S(2)}) collective-permute-start(f32[3,8,1,128]{3,2,1,0:T(1,128)S(1)} %get-tuple-element.380), channel_id=1, source_target_pairs={{4,0},{8,4},{12,8},{16,12},{20,16},{24,20},{28,24},{5,1},{9,5},{13... | collective-permute-start | bytes 36872 | tf_op jit(solution)/shard_map/ppermute | solution.py:26
  22.4 2.7 %copy-start.1 = (f32[24,24]{1,0:T(8,128)S(1)}, f32[24,24]{1,0:T(8,128)}, u32[]{:S(2)}) copy-start(f32[24,24]{1,0:T(8,128)} %param.17) | copy-start | bytes 6916
  22.4 2.7 %copy-start.2 = (f32[24,24]{1,0:T(8,128)S(1)}, f32[24,24]{1,0:T(8,128)}, u32[]{:S(2)}) copy-start(f32[24,24]{1,0:T(8,128)} %param.16) | copy-start | bytes 6916
  22.4 2.8 %collective-permute-start.4 = (f32[3,1,10,128]{3,2,1,0:T(8,128)S(1)}, f32[3,1,10,128]{3,2,1,0:T(8,128)S(1)}, u32[]{:S(2)}, u32[]{:S(2)}) collective-permute-start(f32[3,1,10,128]{3,2,1,0:T(8,128)S(1)} %get-tuple-element.372), channel_id=1, source_target_pairs={{0,1},{1,2},{2,3},{4,5},{5,6},{6,7},{8,9},{9,10},{10,11},{12,13},{... | collective-permute-start | bytes 46088 | tf_op jit(solution)/shard_map/ppermute | solution.py:23
  23.8 7.2 %collective-permute-start.5 = (f32[3,1,10,128]{3,2,1,0:T(8,128)S(1)}, f32[3,1,10,128]{3,2,1,0:T(8,128)S(1)}, u32[]{:S(2)}, u32[]{:S(2)}) collective-permute-start(f32[3,1,10,128]{3,2,1,0:T(8,128)S(1)} %get-tuple-element.371), channel_id=1, source_target_pairs={{1,0},{2,1},{3,2},{5,4},{6,5},{7,6},{9,8},{10,9},{11,10},{13,12},{... | collective-permute-start | bytes 46088 | tf_op jit(solution)/shard_map/ppermute | solution.py:26
  85.5 5.6 %collective-permute-start.6 = (f32[3,8,1,128]{3,2,1,0:T(1,128)S(1)}, f32[3,8,1,128]{3,2,1,0:T(1,128)S(1)}, u32[]{:S(2)}, u32[]{:S(2)}) collective-permute-start(f32[3,8,1,128]{3,2,1,0:T(1,128)S(1)} %get-tuple-element.377), channel_id=1, source_target_pairs={{0,4},{4,8},{8,12},{12,16},{16,20},{20,24},{24,28},{1,5},{5,9},{9,... | collective-permute-start | bytes 36872 | tf_op jit(solution)/shard_map/ppermute | solution.py:23
  89.6 5.6 %collective-permute-start.7 = (f32[3,8,1,128]{3,2,1,0:T(1,128)S(1)}, f32[3,8,1,128]{3,2,1,0:T(1,128)S(1)}, u32[]{:S(2)}, u32[]{:S(2)}) collective-permute-start(f32[3,8,1,128]{3,2,1,0:T(1,128)S(1)} %get-tuple-element.378), channel_id=1, source_target_pairs={{4,0},{8,4},{12,8},{16,12},{20,16},{24,20},{28,24},{5,1},{9,5},{13... | collective-permute-start | bytes 36872 | tf_op jit(solution)/shard_map/ppermute | solution.py:26
  95.2 2.6 %collective-permute-start.8 = (f32[3,1,10,128]{3,2,1,0:T(8,128)S(1)}, f32[3,1,10,128]{3,2,1,0:T(8,128)S(1)}, u32[]{:S(2)}, u32[]{:S(2)}) collective-permute-start(f32[3,1,10,128]{3,2,1,0:T(8,128)S(1)} %get-tuple-element.368), channel_id=1, source_target_pairs={{0,1},{1,2},{2,3},{4,5},{5,6},{6,7},{8,9},{9,10},{10,11},{12,13},{... | collective-permute-start | bytes 46088 | tf_op jit(solution)/shard_map/ppermute | solution.py:23
  96.5 3.5 %collective-permute-start.9 = (f32[3,1,10,128]{3,2,1,0:T(8,128)S(1)}, f32[3,1,10,128]{3,2,1,0:T(8,128)S(1)}, u32[]{:S(2)}, u32[]{:S(2)}) collective-permute-start(f32[3,1,10,128]{3,2,1,0:T(8,128)S(1)} %get-tuple-element.367), channel_id=1, source_target_pairs={{1,0},{2,1},{3,2},{5,4},{6,5},{7,6},{9,8},{10,9},{11,10},{13,12},{... | collective-permute-start | bytes 46088 | tf_op jit(solution)/shard_map/ppermute | solution.py:26
  157.4 5.6 %collective-permute-start.10 = (f32[3,8,1,128]{3,2,1,0:T(1,128)S(1)}, f32[3,8,1,128]{3,2,1,0:T(1,128)S(1)}, u32[]{:S(2)}, u32[]{:S(2)}) collective-permute-start(f32[3,8,1,128]{3,2,1,0:T(1,128)S(1)} %get-tuple-element.375), channel_id=1, source_target_pairs={{0,4},{4,8},{8,12},{12,16},{16,20},{20,24},{24,28},{1,5},{5,9},{9,... | collective-permute-start | bytes 36872 | tf_op jit(solution)/shard_map/ppermute | solution.py:23
  161.6 5.6 %collective-permute-start.11 = (f32[3,8,1,128]{3,2,1,0:T(1,128)S(1)}, f32[3,8,1,128]{3,2,1,0:T(1,128)S(1)}, u32[]{:S(2)}, u32[]{:S(2)}) collective-permute-start(f32[3,8,1,128]{3,2,1,0:T(1,128)S(1)} %get-tuple-element.376), channel_id=1, source_target_pairs={{4,0},{8,4},{12,8},{16,12},{20,16},{24,20},{28,24},{5,1},{9,5},{13... | collective-permute-start | bytes 36872 | tf_op jit(solution)/shard_map/ppermute | solution.py:26
  167.2 2.6 %collective-permute-start.12 = (f32[3,1,10,128]{3,2,1,0:T(8,128)S(1)}, f32[3,1,10,128]{3,2,1,0:T(8,128)S(1)}, u32[]{:S(2)}, u32[]{:S(2)}) collective-permute-start(f32[3,1,10,128]{3,2,1,0:T(8,128)S(1)} %get-tuple-element.364), channel_id=1, source_target_pairs={{0,1},{1,2},{2,3},{4,5},{5,6},{6,7},{8,9},{9,10},{10,11},{12,13},{... | collective-permute-start | bytes 46088 | tf_op jit(solution)/shard_map/ppermute | solution.py:23
  168.5 3.6 %collective-permute-start.13 = (f32[3,1,10,128]{3,2,1,0:T(8,128)S(1)}, f32[3,1,10,128]{3,2,1,0:T(8,128)S(1)}, u32[]{:S(2)}, u32[]{:S(2)}) collective-permute-start(f32[3,1,10,128]{3,2,1,0:T(8,128)S(1)} %get-tuple-element.363), channel_id=1, source_target_pairs={{1,0},{2,1},{3,2},{5,4},{6,5},{7,6},{9,8},{10,9},{11,10},{13,12},{... | collective-permute-start | bytes 46088 | tf_op jit(solution)/shard_map/ppermute | solution.py:26
where the time goes:
time: 231 us; the launch traced here: 229 us
  blocking collectives  129 us (56%)
  starting transfers between devices  30.9 us (13%)
  waiting for transfers between devices  25.7 us (11%)
  local copies, waits for them, and re-layouts  12.1 us (5%)
  between operations  10.5 us (5%)
  other arithmetic  9.69 us (4%)
  matrix products  7.21 us (3%)
  loops' own time  4.67 us (2%)
    psum x3, blocking collectives, inner_sums(): lax.psum((jnp.sum(residual * residual), jnp.sum(residual * image)), ('cur...  129 us
    ppermute x6, waiting for transfers between devices, padded(): lax.ppermute(lax.slice_in_dim(block, 0, width, axis=dim), axis, backward)  23.3 us
    ppermute x6, starting transfers between devices, padded(): lax.ppermute(lax.slice_in_dim(block, block.shape[dim] - width, None, axis...  16.5 us
    ppermute x6, starting transfers between devices, padded(): lax.ppermute(lax.slice_in_dim(block, 0, width, axis=dim), axis, backward)  7.75 us
    dot_general x27, matrix products, layer(): jnp.dot(k_both, scaled, precision=lax.Precision.HIGHEST, preferred_elemen...  7.21 us
    ppermute x2, starting transfers between devices, shifted(): return lax.ppermute(value, axis, pairs)  6.61 us
    another operation x3, loops' own time, node_forces(): _, emitted = lax.scan(layer, start, (lower, upper, layer_coef))  4.67 us
  transfers between devices with their start and end apart: 14, of which 11 were waited for; matrix products, arithmetic and copies ran while one was open for 0% of the time, Pallas kernels for 0%

commit v1 on v0

--- a/solution.py
+++ b/solution.py
@@ -110,7 +110,9 @@
 
 
 def inner_sums(residual, image):
-    return lax.psum((jnp.sum(residual * residual), jnp.sum(residual * image)), ("curve", "sub"))
+    return lax.psum(
+        lax.psum((jnp.sum(residual * residual), jnp.sum(residual * image)), "sub"), "curve"
+    )
 
 
 def local(load, plastic, tile_material, moduli, k_vol, k_dev):

time: 231 us -> 185 us (0.80)
  blocking collectives: 129 us -> 85.6 us
  starting transfers between devices: 30.9 us -> 26 us
  waiting for transfers between devices: 25.7 us -> 28.4 us
    psum x3 -> x6, blocking collectives: 129 us -> 85.6 us  [the longest x3 59.1 us: inner_sums(): lax.psum(lax.psum((jnp.sum(residual * residual), jnp.sum(residual * image...]
    ppermute x6, starting transfers between devices: 16.5 us -> 11.6 us  [padded(): lax.ppermute(lax.slice_in_dim(block, block.shape[dim] - width, None, axis...]
    ppermute x6, waiting for transfers between devices: 23.3 us -> 26.1 us  [padded(): lax.ppermute(lax.slice_in_dim(block, 0, width, axis=dim), axis, backward)]
where the time goes in v1:
time: 185 us; the launch traced here: 184 us
  blocking collectives  85.6 us (46%)
  waiting for transfers between devices  28.4 us (15%)
  starting transfers between devices  26 us (14%)
  local copies, waits for them, and re-layouts  12.1 us (7%)
  between operations  10.6 us (6%)
  other arithmetic  9.67 us (5%)
  matrix products  7.21 us (4%)
  loops' own time  4.67 us (3%)
    psum x3, blocking collectives, inner_sums(): lax.psum(lax.psum((jnp.sum(residual * residual), jnp.sum(residual * image...  59.1 us
    psum x3, blocking collectives, inner_sums(): lax.psum((jnp.sum(residual * residual), jnp.sum(residual * image)), 'sub')  26.5 us
    ppermute x6, waiting for transfers between devices, padded(): lax.ppermute(lax.slice_in_dim(block, 0, width, axis=dim), axis, backward)  26.1 us
    ppermute x6, starting transfers between devices, padded(): lax.ppermute(lax.slice_in_dim(block, block.shape[dim] - width, None, axis...  11.6 us
    ppermute x6, starting transfers between devices, padded(): lax.ppermute(lax.slice_in_dim(block, 0, width, axis=dim), axis, backward)  7.75 us
    dot_general x27, matrix products, layer(): jnp.dot(k_both, scaled, precision=lax.Precision.HIGHEST, preferred_elemen...  7.21 us
    ppermute x2, starting transfers between devices, shifted(): return lax.ppermute(value, axis, pairs)  6.61 us
    another operation x3, loops' own time, node_forces(): _, emitted = lax.scan(layer, start, (lower, upper, layer_coef))  4.67 us
  transfers between devices with their start and end apart: 14, of which 11 were waited for; matrix products, arithmetic and copies ran while one was open for 0% of the time, Pallas kernels for 0%

profile of v1, /device:TPU:0, one launch (start us, length us, event | category | flops | bytes accessed | tf_op | source)
XLA Modules:
  0.0 184.2 jit_solution(10038840336318845124)
XLA Ops:
  2.4 2.4 %collective-permute-start = (f32[2,1,8,128]{3,2,0,1:T(8,128)S(1)}, f32[2,1,8,128]{3,2,0,1:T(8,128)S(1)}, u32[]{:S(2)}, u32[]{:S(2)}) collective-permute-start(f32[2,1,8,128]{3,2,0,1:T(8,128)S(1)} %pad_maximum_fusion.12), channel_id=1, source_target_pairs={{0,1},{1,2},{2,3},{4,5},{5,6},{6,7},{8,9},{9,10},{10,11},{12,13},{... | collective-permute-start | bytes 24584 | tf_op jit(solution)/shard_map/ppermute | solution.py:15
  5.6 4.2 %collective-permute-start.1 = (f32[2,9,1,128]{3,2,0,1:T(1,128)S(1)}, f32[2,9,1,128]{3,2,0,1:T(1,128)S(1)}, u32[]{:S(2)}, u32[]{:S(2)}) collective-permute-start(f32[2,9,1,128]{3,2,0,1:T(1,128)S(1)} %pad_maximum_fusion.10), channel_id=1, source_target_pairs={{0,4},{4,8},{8,12},{12,16},{16,20},{20,24},{24,28},{1,5},{5,9},{9,... | collective-permute-start | bytes 27656 | tf_op jit(solution)/shard_map/ppermute | solution.py:15
  9.8 1.3 collective-permute-done.1
  12.2 4.2 %collective-permute-start.2 = (f32[3,8,1,128]{3,2,1,0:T(1,128)S(1)}, f32[3,8,1,128]{3,2,1,0:T(1,128)S(1)}, u32[]{:S(2)}, u32[]{:S(2)}) collective-permute-start(f32[3,8,1,128]{3,2,1,0:T(1,128)S(1)} %get-tuple-element.385), channel_id=1, source_target_pairs={{0,4},{4,8},{8,12},{12,16},{16,20},{20,24},{24,28},{1,5},{5,9},{9,... | collective-permute-start | bytes 36872 | tf_op jit(solution)/shard_map/ppermute | solution.py:23
  16.4 1.3 collective-permute-start.3
  17.7 4.6 %collective-permute-done.3 = f32[3,8,1,128]{3,2,1,0:T(1,128)S(1)} collective-permute-done((f32[3,8,1,128]{3,2,1,0:T(1,128)S(1)}, f32[3,8,1,128]{3,2,1,0:T(1,128)S(1)}, u32[]{:S(2)}, u32[]{:S(2)}) %collective-permute-start.3) | collective-permute-done | bytes 12320 | tf_op jit(solution)/shard_map/ppermute | solution.py:26
  22.4 1.4 collective-permute-start.4
  23.8 1.3 collective-permute-start.5
  25.2 5.8 %collective-permute-done.5 = f32[3,1,10,128]{3,2,1,0:T(8,128)S(1)} collective-permute-done((f32[3,1,10,128]{3,2,1,0:T(8,128)S(1)}, f32[3,1,10,128]{3,2,1,0:T(8,128)S(1)}, u32[]{:S(2)}, u32[]{:S(2)}) %collective-permute-start.5) | collective-permute-done | bytes 15392 | tf_op jit(solution)/shard_map/ppermute | solution.py:26
  31.0 9.3 %while.39 = (s32[]{:T(128)}, f32[3,8,128]{2,1,0:T(8,128)S(1)}, f32[9,3,8,128]{3,2,0,1:T(8,128)S(1)}, f32[9,2,9,128]{3,2,1,0:T(8,128)S(1)}, f32[9,3,10,128]{3,2,0...) while((s32[]{:T(128)}, f32[3,8,128]{2,1,0:T(8,128)S(1)}, ...), condition=%wide.region_5.6_spmd.clone, body=%wide.region_4.5_spmd.clone.sunk | while | flops 16060420 | bytes 1924459 | solution.py:108
  40.9 8.8 %all-reduce.33 = (f32[]{:T(128)}, f32[]{:T(128)}) all-reduce(f32[]{:T(128)} %get-tuple-element.256, f32[]{:T(128)} %get-tuple-element.255), channel_id=1, replica_groups=mesh['curve'=8,'sub'=4] {'sub'}, use_global_device_ids=true, to_apply=%region_2.3 | all-reduce | flops 2 | bytes 16 | tf_op jit(solution)/shard_map/psum | solution.py:114
  49.8 20.9 %all-reduce.30 = (f32[]{:T(128)}, f32[]{:T(128)}) all-reduce(f32[]{:T(128)} %get-tuple-element.309, f32[]{:T(128)} %get-tuple-element.310), channel_id=1, replica_groups=mesh['curve'=8,'sub'=4] {'curve'}, use_global_device_ids=true, to_apply=%region_3.4 | all-reduce | flops 2 | bytes 16 | tf_op jit(solution)/shard_map/psum | solution.py:113
  73.3 1.3 collective-permute-start.7
  74.7 4.2 %collective-permute-done.7 = f32[3,8,1,128]{3,2,1,0:T(1,128)S(1)} collective-permute-done((f32[3,8,1,128]{3,2,1,0:T(1,128)S(1)}, f32[3,8,1,128]{3,2,1,0:T(1,128)S(1)}, u32[]{:S(2)}, u32[]{:S(2)}) %collective-permute-start.7) | collective-permute-done | bytes 12320 | tf_op jit(solution)/shard_map/ppermute | solution.py:26
  81.6 3.6 %collective-permute-done.9 = f32[3,1,10,128]{3,2,1,0:T(8,128)S(1)} collective-permute-done((f32[3,1,10,128]{3,2,1,0:T(8,128)S(1)}, f32[3,1,10,128]{3,2,1,0:T(8,128)S(1)}, u32[]{:S(2)}, u32[]{:S(2)}) %collective-permute-start.9) | collective-permute-done | bytes 15392 | tf_op jit(solution)/shard_map/ppermute | solution.py:26
  85.3 9.3 %while.40 = (s32[]{:T(128)}, f32[3,8,128]{2,1,0:T(8,128)S(1)}, f32[9,3,8,128]{3,2,0,1:T(8,128)S(1)}, f32[9,2,9,128]{3,2,1,0:T(8,128)S(1)}, f32[9,3,10,128]{3,2,0...) while((s32[]{:T(128)}, f32[3,8,128]{2,1,0:T(8,128)S(1)}, ...), condition=%wide.region_13.14_spmd.clone, body=%wide.region_12.13_spmd.clone.sunk | while | flops 16060420 | bytes 1924459 | solution.py:108
  95.2 8.9 %all-reduce.32 = (f32[]{:T(128)}, f32[]{:T(128)}) all-reduce(f32[]{:T(128)} %get-tuple-element.254, f32[]{:T(128)} %get-tuple-element.253), channel_id=1, replica_groups=mesh['curve'=8,'sub'=4] {'sub'}, use_global_device_ids=true, to_apply=%region_10.11 | all-reduce | flops 2 | bytes 16 | tf_op jit(solution)/shard_map/psum | solution.py:114
  104.1 19.5 %all-reduce.29 = (f32[]{:T(128)}, f32[]{:T(128)}) all-reduce(f32[]{:T(128)} %get-tuple-element.307, f32[]{:T(128)} %get-tuple-element.308), channel_id=1, replica_groups=mesh['curve'=8,'sub'=4] {'curve'}, use_global_device_ids=true, to_apply=%region_11.12 | all-reduce | flops 2 | bytes 16 | tf_op jit(solution)/shard_map/psum | solution.py:113
  128.2 2.2 %collective-permute-start.10 = (f32[3,8,1,128]{3,2,1,0:T(1,128)S(1)}, f32[3,8,1,128]{3,2,1,0:T(1,128)S(1)}, u32[]{:S(2)}, u32[]{:S(2)}) collective-permute-start(f32[3,8,1,128]{3,2,1,0:T(1,128)S(1)} %get-tuple-element.381), channel_id=1, source_target_pairs={{0,4},{4,8},{8,12},{12,16},{16,20},{20,24},{24,28},{1,5},{5,9},{9,... | collective-permute-start | bytes 36872 | tf_op jit(solution)/shard_map/ppermute | solution.py:23
  131.7 4.2 %collective-permute-done.11 = f32[3,8,1,128]{3,2,1,0:T(1,128)S(1)} collective-permute-done((f32[3,8,1,128]{3,2,1,0:T(1,128)S(1)}, f32[3,8,1,128]{3,2,1,0:T(1,128)S(1)}, u32[]{:S(2)}, u32[]{:S(2)}) %collective-permute-start.11) | collective-permute-done | bytes 12320 | tf_op jit(solution)/shard_map/ppermute | solution.py:26
  138.6 3.6 %collective-permute-done.13 = f32[3,1,10,128]{3,2,1,0:T(8,128)S(1)} collective-permute-done((f32[3,1,10,128]{3,2,1,0:T(8,128)S(1)}, f32[3,1,10,128]{3,2,1,0:T(8,128)S(1)}, u32[]{:S(2)}, u32[]{:S(2)}) %collective-permute-start.13) | collective-permute-done | bytes 15392 | tf_op jit(solution)/shard_map/ppermute | solution.py:26
  142.3 9.3 %while.41 = (s32[]{:T(128)}, f32[3,8,128]{2,1,0:T(8,128)S(1)}, f32[9,3,8,128]{3,2,0,1:T(8,128)S(1)}, f32[9,2,9,128]{3,2,1,0:T(8,128)S(1)}, f32[9,3,10,128]{3,2,0...) while((s32[]{:T(128)}, f32[3,8,128]{2,1,0:T(8,128)S(1)}, ...), condition=%wide.region_21.22_spmd.clone, body=%wide.region_20.21_spmd.clone.sunk | while | flops 16060420 | bytes 1924459 | solution.py:108
  152.2 8.8 %all-reduce.31 = (f32[]{:T(128)}, f32[]{:T(128)}) all-reduce(f32[]{:T(128)} %get-tuple-element.252, f32[]{:T(128)} %get-tuple-element.251), channel_id=1, replica_groups=mesh['curve'=8,'sub'=4] {'sub'}, use_global_device_ids=true, to_apply=%region_18.19 | all-reduce | flops 2 | bytes 16 | tf_op jit(solution)/shard_map/psum | solution.py:114
  161.0 18.7 %all-reduce.28 = (f32[]{:T(128)}, f32[]{:T(128)}) all-reduce(f32[]{:T(128)} %get-tuple-element.305, f32[]{:T(128)} %get-tuple-element.306), channel_id=1, replica_groups=mesh['curve'=8,'sub'=4] {'curve'}, use_global_device_ids=true, to_apply=%region_19.20 | all-reduce | flops 2 | bytes 16 | tf_op jit(solution)/shard_map/psum | solution.py:113
  (844 shorter events, 37.7 us)
Async XLA Ops:
  0.6 0.7 copy-start.3
  0.7 0.7 copy-start.4
  2.4 3.2 %collective-permute-start = (f32[2,1,8,128]{3,2,0,1:T(8,128)S(1)}, f32[2,1,8,128]{3,2,0,1:T(8,128)S(1)}, u32[]{:S(2)}, u32[]{:S(2)}) collective-permute-start(f32[2,1,8,128]{3,2,0,1:T(8,128)S(1)} %pad_maximum_fusion.12), channel_id=1, source_target_pairs={{0,1},{1,2},{2,3},{4,5},{5,6},{6,7},{8,9},{9,10},{10,11},{12,13},{... | collective-permute-start | bytes 24584 | tf_op jit(solution)/shard_map/ppermute | solution.py:15
  5.6 5.6 %collective-permute-start.1 = (f32[2,9,1,128]{3,2,0,1:T(1,128)S(1)}, f32[2,9,1,128]{3,2,0,1:T(1,128)S(1)}, u32[]{:S(2)}, u32[]{:S(2)}) collective-permute-start(f32[2,9,1,128]{3,2,0,1:T(1,128)S(1)} %pad_maximum_fusion.10), channel_id=1, source_target_pairs={{0,4},{4,8},{8,12},{12,16},{16,20},{20,24},{24,28},{1,5},{5,9},{9,... | collective-permute-start | bytes 27656 | tf_op jit(solution)/shard_map/ppermute | solution.py:15
  11.2 0.9 copy-start
  12.2 5.6 %collective-permute-start.2 = (f32[3,8,1,128]{3,2,1,0:T(1,128)S(1)}, f32[3,8,1,128]{3,2,1,0:T(1,128)S(1)}, u32[]{:S(2)}, u32[]{:S(2)}) collective-permute-start(f32[3,8,1,128]{3,2,1,0:T(1,128)S(1)} %get-tuple-element.385), channel_id=1, source_target_pairs={{0,4},{4,8},{8,12},{12,16},{16,20},{20,24},{24,28},{1,5},{5,9},{9,... | collective-permute-start | bytes 36872 | tf_op jit(solution)/shard_map/ppermute | solution.py:23
  16.4 6.0 %collective-permute-start.3 = (f32[3,8,1,128]{3,2,1,0:T(1,128)S(1)}, f32[3,8,1,128]{3,2,1,0:T(1,128)S(1)}, u32[]{:S(2)}, u32[]{:S(2)}) collective-permute-start(f32[3,8,1,128]{3,2,1,0:T(1,128)S(1)} %get-tuple-element.386), channel_id=1, source_target_pairs={{4,0},{8,4},{12,8},{16,12},{20,16},{24,20},{28,24},{5,1},{9,5},{13... | collective-permute-start | bytes 36872 | tf_op jit(solution)/shard_map/ppermute | solution.py:26
  22.4 2.7 %copy-start.1 = (f32[24,24]{1,0:T(8,128)S(1)}, f32[24,24]{1,0:T(8,128)}, u32[]{:S(2)}) copy-start(f32[24,24]{1,0:T(8,128)} %param.17) | copy-start | bytes 6916
  22.4 2.7 %copy-start.2 = (f32[24,24]{1,0:T(8,128)S(1)}, f32[24,24]{1,0:T(8,128)}, u32[]{:S(2)}) copy-start(f32[24,24]{1,0:T(8,128)} %param.16) | copy-start | bytes 6916
  22.4 2.8 %collective-permute-start.4 = (f32[3,1,10,128]{3,2,1,0:T(8,128)S(1)}, f32[3,1,10,128]{3,2,1,0:T(8,128)S(1)}, u32[]{:S(2)}, u32[]{:S(2)}) collective-permute-start(f32[3,1,10,128]{3,2,1,0:T(8,128)S(1)} %get-tuple-element.378), channel_id=1, source_target_pairs={{0,1},{1,2},{2,3},{4,5},{5,6},{6,7},{8,9},{9,10},{10,11},{12,13},{... | collective-permute-start | bytes 46088 | tf_op jit(solution)/shard_map/ppermute | solution.py:23
  23.8 7.2 %collective-permute-start.5 = (f32[3,1,10,128]{3,2,1,0:T(8,128)S(1)}, f32[3,1,10,128]{3,2,1,0:T(8,128)S(1)}, u32[]{:S(2)}, u32[]{:S(2)}) collective-permute-start(f32[3,1,10,128]{3,2,1,0:T(8,128)S(1)} %get-tuple-element.377), channel_id=1, source_target_pairs={{1,0},{2,1},{3,2},{5,4},{6,5},{7,6},{9,8},{10,9},{11,10},{13,12},{... | collective-permute-start | bytes 46088 | tf_op jit(solution)/shard_map/ppermute | solution.py:26
  72.0 2.7 %collective-permute-start.6 = (f32[3,8,1,128]{3,2,1,0:T(1,128)S(1)}, f32[3,8,1,128]{3,2,1,0:T(1,128)S(1)}, u32[]{:S(2)}, u32[]{:S(2)}) collective-permute-start(f32[3,8,1,128]{3,2,1,0:T(1,128)S(1)} %get-tuple-element.383), channel_id=1, source_target_pairs={{0,4},{4,8},{8,12},{12,16},{16,20},{20,24},{24,28},{1,5},{5,9},{9,... | collective-permute-start | bytes 36872 | tf_op jit(solution)/shard_map/ppermute | solution.py:23
  73.3 5.6 %collective-permute-start.7 = (f32[3,8,1,128]{3,2,1,0:T(1,128)S(1)}, f32[3,8,1,128]{3,2,1,0:T(1,128)S(1)}, u32[]{:S(2)}, u32[]{:S(2)}) collective-permute-start(f32[3,8,1,128]{3,2,1,0:T(1,128)S(1)} %get-tuple-element.384), channel_id=1, source_target_pairs={{4,0},{8,4},{12,8},{16,12},{20,16},{24,20},{28,24},{5,1},{9,5},{13... | collective-permute-start | bytes 36872 | tf_op jit(solution)/shard_map/ppermute | solution.py:26
  78.9 2.6 %collective-permute-start.8 = (f32[3,1,10,128]{3,2,1,0:T(8,128)S(1)}, f32[3,1,10,128]{3,2,1,0:T(8,128)S(1)}, u32[]{:S(2)}, u32[]{:S(2)}) collective-permute-start(f32[3,1,10,128]{3,2,1,0:T(8,128)S(1)} %get-tuple-element.374), channel_id=1, source_target_pairs={{0,1},{1,2},{2,3},{4,5},{5,6},{6,7},{8,9},{9,10},{10,11},{12,13},{... | collective-permute-start | bytes 46088 | tf_op jit(solution)/shard_map/ppermute | solution.py:23
  80.2 5.0 %collective-permute-start.9 = (f32[3,1,10,128]{3,2,1,0:T(8,128)S(1)}, f32[3,1,10,128]{3,2,1,0:T(8,128)S(1)}, u32[]{:S(2)}, u32[]{:S(2)}) collective-permute-start(f32[3,1,10,128]{3,2,1,0:T(8,128)S(1)} %get-tuple-element.373), channel_id=1, source_target_pairs={{1,0},{2,1},{3,2},{5,4},{6,5},{7,6},{9,8},{10,9},{11,10},{13,12},{... | collective-permute-start | bytes 46088 | tf_op jit(solution)/shard_map/ppermute | solution.py:26
  128.2 3.6 %collective-permute-start.10 = (f32[3,8,1,128]{3,2,1,0:T(1,128)S(1)}, f32[3,8,1,128]{3,2,1,0:T(1,128)S(1)}, u32[]{:S(2)}, u32[]{:S(2)}) collective-permute-start(f32[3,8,1,128]{3,2,1,0:T(1,128)S(1)} %get-tuple-element.381), channel_id=1, source_target_pairs={{0,4},{4,8},{8,12},{12,16},{16,20},{20,24},{24,28},{1,5},{5,9},{9,... | collective-permute-start | bytes 36872 | tf_op jit(solution)/shard_map/ppermute | solution.py:23
  130.4 5.6 %collective-permute-start.11 = (f32[3,8,1,128]{3,2,1,0:T(1,128)S(1)}, f32[3,8,1,128]{3,2,1,0:T(1,128)S(1)}, u32[]{:S(2)}, u32[]{:S(2)}) collective-permute-start(f32[3,8,1,128]{3,2,1,0:T(1,128)S(1)} %get-tuple-element.382), channel_id=1, source_target_pairs={{4,0},{8,4},{12,8},{16,12},{20,16},{24,20},{28,24},{5,1},{9,5},{13... | collective-permute-start | bytes 36872 | tf_op jit(solution)/shard_map/ppermute | solution.py:26
  136.0 2.6 %collective-permute-start.12 = (f32[3,1,10,128]{3,2,1,0:T(8,128)S(1)}, f32[3,1,10,128]{3,2,1,0:T(8,128)S(1)}, u32[]{:S(2)}, u32[]{:S(2)}) collective-permute-start(f32[3,1,10,128]{3,2,1,0:T(8,128)S(1)} %get-tuple-element.370), channel_id=1, source_target_pairs={{0,1},{1,2},{2,3},{4,5},{5,6},{6,7},{8,9},{9,10},{10,11},{12,13},{... | collective-permute-start | bytes 46088 | tf_op jit(solution)/shard_map/ppermute | solution.py:23
  137.3 5.0 %collective-permute-start.13 = (f32[3,1,10,128]{3,2,1,0:T(8,128)S(1)}, f32[3,1,10,128]{3,2,1,0:T(8,128)S(1)}, u32[]{:S(2)}, u32[]{:S(2)}) collective-permute-start(f32[3,1,10,128]{3,2,1,0:T(8,128)S(1)} %get-tuple-element.369), channel_id=1, source_target_pairs={{1,0},{2,1},{3,2},{5,4},{6,5},{7,6},{9,8},{10,9},{11,10},{13,12},{... | collective-permute-start | bytes 46088 | tf_op jit(solution)/shard_map/ppermute | solution.py:26
